TPU v7x, 32 devices: a whole 2x2x4 slice. The times are simulated.
32 devices in a mesh: dp: 2 (over x), head: 16 (over z, y, core).
Axes of the slice: x: 2, y: 2, z: 4, core: 2. Of those that a mesh axis runs over, the one named last changes fastest.
Arguments:
- queries: bfloat16 [2048, 8192], P('dp', 'head'), may hold values from -14 to 14
- keys: bfloat16 [2048, 8192], P('dp', 'head'), may hold values from -14 to 14
- values: bfloat16 [2048, 8192], P('dp', 'head'), may hold values from -24 to 24
Outputs:
- regrouped: bfloat16 [2048, 8192], P(('dp', 'head'))
- hessian: float32 [8192, 8192], P('dp', 'head')
All inputs are finite; a program needn't handle non-finite values.
Results may differ from a plain program's by a relative error of at most 0.0044.
Values may be sent and summed in bfloat16 or wider, within the bound.
A program may use at most 128 MiB of HBM per device.

v0:
```python
import math

import jax
import jax.numpy as jnp
from jax import lax
from jax.sharding import PartitionSpec as P

HEAD_SIZE = 128


def attend(queries, keys, values):
    rows_local = queries.shape[0]
    heads_local = queries.shape[1] // HEAD_SIZE
    query_heads = queries.reshape(rows_local, heads_local, HEAD_SIZE)
    key_heads = keys.reshape(rows_local, heads_local, HEAD_SIZE)
    value_heads = values.reshape(rows_local, heads_local, HEAD_SIZE)
    logit_matrix = jnp.einsum(
        "qhd,khd->hqk", query_heads, key_heads, preferred_element_type=jnp.float32
    ) * (1.0 / math.sqrt(HEAD_SIZE))
    causal = lax.broadcasted_iota(jnp.int32, (rows_local, rows_local), 0) >= lax.broadcasted_iota(
        jnp.int32, (rows_local, rows_local), 1
    )
    logit_matrix = jnp.where(causal[None], logit_matrix, -1e30)
    peak = jnp.max(logit_matrix, axis=-1, keepdims=True)
    raised = jnp.exp(logit_matrix - peak)
    attention_weight = (raised / jnp.sum(raised, axis=-1, keepdims=True)).astype(jnp.bfloat16)
    attended_values = jnp.einsum(
        "hqk,khd->qhd", attention_weight, value_heads, preferred_element_type=jnp.float32
    )
    return attended_values.astype(jnp.bfloat16).reshape(rows_local, heads_local * HEAD_SIZE)


def gram_block(left_part, right_part):
    return lax.dot_general(
        left_part, right_part, (((0,), (0,)), ((), ())), preferred_element_type=jnp.float32
    )


def body(queries, keys, values):
    outputs = attend(queries, keys, values)
    rows_local = outputs.shape[0]
    regrouped = lax.all_to_all(outputs, "head", split_axis=0, concat_axis=1, tiled=True)
    term = gram_block(lax.all_gather(outputs, "head", axis=1, tiled=True), outputs)
    summed = lax.psum_scatter(term, "dp", scatter_dimension=0, tiled=True)
    tokens_all = rows_local * lax.axis_size("dp")
    hessian = summed * (2.0 / tokens_all)
    return (regrouped, hessian)


def solution(mesh):
    in_specs = (P("dp", "head"), P("dp", "head"), P("dp", "head"))
    out_specs = (P(("dp", "head"), None), P("dp", "head"))
    return jax.shard_map(body, mesh=mesh, in_specs=in_specs, out_specs=out_specs, check_vma=False)
```

profile of v0, /device:TPU:0, one launch (start us, length us, event | category | flops | bytes accessed | tf_op | source)
XLA Modules:
  0.0 375.5 jit_solution(3450220839177552944)
XLA Ops:
  7.2 0.0 copy-start
  7.2 0.0 all-gather.2.cloned.1.call-start
  7.2 0.3 iota_compare_fusion
  7.5 1.5 copy.22
  9.0 0.0 copy-done
  9.0 10.9 %fusion.30 = (f32[4,1024]{1,0:T(4,128)S(1)}, f32[4,1024,1024]{1,2,0:T(8,128)}) fusion(pred[1024,1024]{0,1:T(8,128)(4,1)S(1)} %iota_compare_fusion, bf16[1024,512]{1,0:T(8,128)(2,1)S(1)} %copy-done, bf16[1024,512]{1,0:T(8,128)(2,1)} %param.3), kind=kOutput, calls=%fused_computation.24 | convolution fusion | flops 1090520064 | bytes 19939328 | tf_op jit(solution)/shard_map/sub | solution.py:25
  20.0 8.0 %fusion.8 = bf16[4,1024,128]{1,2,0:T(8,128)(2,1)} fusion(bf16[1024,4,128]{0,2,1:T(8,128)(2,1)S(1)} %bitcast.55, f32[4,1024,1024]{1,2,0:T(8,128)} %get-tuple-element.3, f32[4,1024]{1,0:T(4,128)S(1)} %get-tuple-element.2), kind=kOutput, calls=%fused_computation.12 | convolution fusion | flops 1082654720 | bytes 18890752 | tf_op jit(solution)/shard_map/hqk,khd->qhd/dot_general | solution.py:27
  28.0 0.0 all-gather.2.cloned.1.call-update
  28.0 0.0 reduce-scatter.2.cloned.1.call-start
  28.1 129.3 %all-gather.2.cloned.1.call-done = bf16[1024,8192]{0,1:T(8,128)(2,1)} async-done(((bf16[1024,512]{0,1:T(8,128)(2,1)}), bf16[1024,8192]{0,1:T(8,128)(2,1)}) %all-gather.2.cloned.1.call-update) | async-done | bytes 16777232 | tf_op jit(solution)/shard_map/all_gather | solution.py:43
  157.3 16.0 %fusion.39 = f32[8192,512]{1,0:T(8,128)} fusion(bf16[1024,8192]{0,1:T(8,128)(2,1)} %all-gather.2.cloned.1.call-done, bf16[1024,512]{0,1:T(8,128)(2,1)} %bitcast.51), kind=kOutput, calls=%fused_computation.25 | convolution fusion | flops 8589934592 | bytes 34603008 | tf_op jit(solution)/shard_map/dot_general | solution.py:34
  173.3 0.0 copy-start.2
  173.3 0.0 reduce-scatter.2.cloned.1.call-update
  173.3 0.0 copy-start.1
  173.4 1.2 copy-done.2
  174.5 0.7 copy.19
  175.3 0.4 all_to_all.14
  175.7 27.4 %all_to_all.19 = bf16[16,64,512]{2,1,0:T(8,128)(2,1)S(1)} all-to-all(bf16[16,64,512]{2,1,0:T(8,128)(2,1)S(1)} %all_to_all.14), channel_id=1, replica_groups=mesh['dp'=2,'head'=16] {'head'}, dimensions={0} | all-to-all | bytes 2097152 | tf_op jit(solution)/shard_map/all_to_all | solution.py:42
  203.1 1.1 copy.25
  204.2 156.7 %reduce-scatter.2.cloned.1.call-done = f32[4096,512]{1,0:T(8,128)} async-done(((f32[8192,512]{1,0:T(8,128)}), f32[4096,512]{1,0:T(8,128)}) %reduce-scatter.2.cloned.1.call-update) | async-done | bytes 8388624 | tf_op jit(solution)/shard_map/reduce_scatter | solution.py:44
  360.9 7.8 %broadcast_multiply_fusion = f32[4096,512]{1,0:T(8,128)} fusion(f32[4096,512]{1,0:T(8,128)} %reduce-scatter.2.cloned.1.call-done), kind=kLoop, calls=%fused_computation.9 | loop fusion | flops 2097152 | bytes 16777216 | tf_op jit(solution)/shard_map/mul | solution.py:46
  368.7 0.0 copy-done.1
Async XLA Ops:
  7.2 1.9 copy-start
  7.2 150.2 %all-gather.2.cloned.1.call-start = ((), (), s32[]{:S(2)}) async-start(), calls=%async_computation.2 | async-start | bytes 17825792 | tf_op jit(solution)/shard_map/all_gather | solution.py:43
  28.0 332.9 %reduce-scatter.2.cloned.1.call-start = ((), (), s32[]{:S(2)}) async-start(), calls=%async_computation.3 | async-start | bytes 25165824 | tf_op jit(solution)/shard_map/reduce_scatter | solution.py:44
  173.3 1.2 copy-start.2
  173.3 195.4 %copy-start.1 = (bf16[1024,512]{1,0:T(8,128)(2,1)S(1)}, bf16[1024,512]{1,0:T(8,128)(2,1)}, u32[]{:S(2)}) copy-start(bf16[1024,512]{1,0:T(8,128)(2,1)} %param.4) | copy-start | bytes 3145732
Sparse Core Ops, SparseCore 0:
  28.1 129.1 all-gather.1
  173.5 187.3 reduce-scatter.1
where the time goes:
time: 376 us
  waiting for transfers between devices  286 us (76%)
  matrix products  34.9 us (9%)
  blocking collectives  27.4 us (7%)
  between operations  14.1 us (4%)
  other arithmetic  8.13 us (2%)
  local copies, waits for them, and re-layouts  4.95 us (1%)
    reduce_scatter x1, waiting for transfers between devices, body(): summed = lax.psum_scatter(term, 'dp', scatter_dimension=0, tiled=True)  157 us
    all_gather x1, waiting for transfers between devices, body(): lax.all_gather(outputs, 'head', axis=1, tiled=True)  129 us
    all_to_all x1, blocking collectives, body(): lax.all_to_all(outputs, 'head', split_axis=0, concat_axis=1, tiled=True)  27.4 us
    dot_general x1, matrix products, gram_block(): lax.dot_general(left_part, right_part, (((0,), (0,)), ((), ())), preferre...  16 us
    sub x1, matrix products, attend(): raised = jnp.exp(logit_matrix - peak)  10.9 us
    dot_general x1, matrix products, attend(): jnp.einsum('hqk,khd->qhd', attention_weight, value_heads, preferred_eleme...  8.03 us
    mul x1, other arithmetic, body(): hessian = summed * (2.0 / tokens_all)  7.82 us
  transfers between devices with their start and end apart: 2, of which 2 were waited for; matrix products, arithmetic and copies ran while one was open for 0% of the time, Pallas kernels for 0%

commit v1 on v0

--- a/solution.py
+++ b/solution.py
@@ -30,20 +30,41 @@
     return attended_values.astype(jnp.bfloat16).reshape(rows_local, heads_local * HEAD_SIZE)
 
 
-def gram_block(left_part, right_part):
-    return lax.dot_general(
-        left_part, right_part, (((0,), (0,)), ((), ())), preferred_element_type=jnp.float32
-    )
-
-
 def body(queries, keys, values):
     outputs = attend(queries, keys, values)
-    rows_local = outputs.shape[0]
-    regrouped = lax.all_to_all(outputs, "head", split_axis=0, concat_axis=1, tiled=True)
-    term = gram_block(lax.all_gather(outputs, "head", axis=1, tiled=True), outputs)
-    summed = lax.psum_scatter(term, "dp", scatter_dimension=0, tiled=True)
-    tokens_all = rows_local * lax.axis_size("dp")
-    hessian = summed * (2.0 / tokens_all)
+    rows, cols = outputs.shape
+    groups = lax.axis_size("dp")
+    heads = lax.axis_size("head")
+    me = lax.axis_index("dp")
+    position = lax.axis_index("head")
+    scale = 2.0 / (rows * groups)
+    chunks = 2 if cols % 256 == 0 else 1
+    width = cols // chunks
+    rows_out = rows // heads
+    pieces, sums = [], []
+    for c in range(chunks):
+        part = outputs[:, c * width : (c + 1) * width]
+        gathered = lax.all_gather(part, "head", axis=0, tiled=False)
+        mine = lax.dynamic_slice_in_dim(gathered, position * rows_out, rows_out, axis=1)
+        pieces.append(jnp.swapaxes(mine, 0, 1))
+
+        def term(owner):
+            block = lax.dynamic_slice_in_dim(
+                gathered, owner * (heads // groups), heads // groups, axis=0
+            )
+            return jnp.einsum("htf,tc->hfc", block, outputs, preferred_element_type=jnp.float32)
+
+        arrived = []
+        for shift in range(1, groups):
+            sent = term(lax.rem(me + shift, groups)).astype(jnp.bfloat16)
+            pairs = [(g, (g + shift) % groups) for g in range(groups)]
+            arrived.append(lax.ppermute(sent, "dp", pairs))
+        total = term(me)
+        for other in arrived:
+            total = total + other.astype(jnp.float32)
+        sums.append(total * scale)
+    regrouped = jnp.concatenate(pieces, axis=2).reshape(rows_out, heads * cols)
+    hessian = jnp.concatenate(sums, axis=1).reshape(heads * cols // groups, cols)
     return (regrouped, hessian)
 
 

time: 376 us -> 251 us (0.67)
  waiting for transfers between devices: 286 us -> 182 us
  blocking collectives: 27.4 us -> 0 us
  matrix products: 34.9 us -> 39 us
    reduce_scatter x1 -> x0, waiting for transfers between devices: 157 us -> none  [body(): summed = lax.psum_scatter(term, 'dp', scatter_dimension=0, tiled=True)]
    ppermute x0 -> x2, waiting for transfers between devices: none -> 38.1 us  [body(): arrived.append(lax.ppermute(sent, 'dp', pairs))]
    all_to_all x1 -> x0, blocking collectives: 27.4 us -> none  [body(): lax.all_to_all(outputs, 'head', split_axis=0, concat_axis=1, tiled=True)]
    all_gather x1 -> x2, waiting for transfers between devices: 129 us -> 144 us  [body(): gathered = lax.all_gather(part, 'head', axis=0, tiled=False)]
    mul x1 -> x0, other arithmetic: 7.82 us -> none  [body(): hessian = summed * (2.0 / tokens_all)]
    concatenate x0 -> x1, other arithmetic: none -> 5.1 us  [body(): jnp.concatenate(sums, axis=1).reshape(heads * cols // groups, cols)]
    dot_general x1 -> x4, matrix products: 16 us -> 21 us  [term(): jnp.einsum('htf,tc->hfc', block, outputs, preferred_element_type=jnp.floa...]
  transfers between devices with their start and end apart: 2 -> 4, of which waited for: 2 -> 3; matrix products, arithmetic and copies ran while one was open for 0% -> 9% of each run, Pallas kernels for 0% -> 0%
where the time goes in v1:
time: 251 us; the launch traced here: 250 us
  waiting for transfers between devices  182 us (73%)
  matrix products  39 us (16%)
  between operations  14.2 us (6%)
  local copies, waits for them, and re-layouts  6.83 us (3%)
  other arithmetic  5.49 us (2%)
  starting transfers between devices  3.2 us (1%)
    all_gather x2, waiting for transfers between devices, body(): gathered = lax.all_gather(part, 'head', axis=0, tiled=False)  144 us
    ppermute x2, waiting for transfers between devices, body(): arrived.append(lax.ppermute(sent, 'dp', pairs))  38.1 us
    dot_general x4, matrix products, term(): jnp.einsum('htf,tc->hfc', block, outputs, preferred_element_type=jnp.floa...  21 us
    sub x1, matrix products, attend(): raised = jnp.exp(logit_matrix - peak)  11 us
    dot_general x1, matrix products, attend(): jnp.einsum('hqk,khd->qhd', attention_weight, value_heads, preferred_eleme...  7.06 us
    concatenate x1, other arithmetic, body(): jnp.concatenate(sums, axis=1).reshape(heads * cols // groups, cols)  5.1 us
  transfers between devices with their start and end apart: 4, of which 3 were waited for; matrix products, arithmetic and copies ran while one was open for 9% of the time, Pallas kernels for 0%

profile of v1, /device:TPU:0, one launch (start us, length us, event | category | flops | bytes accessed | tf_op | source)
XLA Modules:
  0.0 250.4 jit_solution(13425893116356748818)
XLA Ops:
  7.2 0.0 copy-start
  7.2 0.0 all-gather.7.cloned.1.call-start
  7.2 0.3 iota_compare_fusion
  7.5 1.5 copy.48
  9.0 0.0 copy-done
  9.0 11.0 %fusion.53 = (f32[4,1024]{1,0:T(4,128)S(1)}, f32[4,1024,1024]{1,2,0:T(8,128)}) fusion(pred[1024,1024]{0,1:T(8,128)(4,1)S(1)} %iota_compare_fusion, bf16[1024,512]{1,0:T(8,128)(2,1)S(1)} %copy-done, bf16[1024,512]{1,0:T(8,128)(2,1)} %param.3), kind=kOutput, calls=%fused_computation.44 | convolution fusion | flops 1090520064 | bytes 19939328 | tf_op jit(solution)/shard_map/sub | solution.py:25
  20.0 7.1 %fusion.26 = bf16[4,1024,128]{1,2,0:T(8,128)(2,1)S(1)} fusion(bf16[1024,4,128]{0,2,1:T(8,128)(2,1)S(1)} %bitcast.71, f32[4,1024,1024]{1,2,0:T(8,128)} %get-tuple-element.7, f32[4,1024]{1,0:T(4,128)S(1)} %get-tuple-element.6), kind=kOutput, calls=%fused_computation.24 | convolution fusion | flops 1082654720 | bytes 18890752 | tf_op jit(solution)/shard_map/hqk,khd->qhd/dot_general | solution.py:27
  27.1 0.1 fusion.52
  27.1 1.0 copy.54
  28.1 0.0 all-gather.7.cloned.1.call-update
  28.2 0.2 all-gather.5.cloned.1.call-start
  28.4 1.0 copy.53
  29.4 0.0 all-gather.5.cloned.1.call-update
  29.4 75.9 %all-gather.7.cloned.1.call-done = bf16[16384,256]{1,0:T(8,128)(2,1)} async-done(((bf16[1024,256]{1,0:T(8,128)(2,1)}), bf16[16384,256]{1,0:T(8,128)(2,1)}) %all-gather.7.cloned.1.call-update) | async-done | bytes 8388624 | tf_op jit(solution)/shard_map/all_gather | solution.py:47
  105.4 5.9 %fusion.21 = bf16[8,256,512]{2,1,0:T(8,128)(2,1)} fusion(bf16[1024,512,1]{0,1,2:T(8,128)(2,1)S(1)} %bitcast.66, bf16[16,1024,256]{2,1,0:T(8,128)(2,1)} %bitcast.72, s32[]{:T(128)S(6)} %select_n.19), kind=kOutput, calls=%fused_computation.22 | convolution fusion | flops 2148532224 | bytes 7340036 | tf_op jit(solution)/shard_map/htf,tc->hfc/dot_general | solution.py:55
  111.3 1.5 collective-permute-start.1
  112.7 67.7 %all-gather.5.cloned.1.call-done = bf16[16384,256]{1,0:T(8,128)(2,1)} async-done(((bf16[1024,256]{1,0:T(8,128)(2,1)}), bf16[16384,256]{1,0:T(8,128)(2,1)}) %all-gather.5.cloned.1.call-update) | async-done | bytes 8388624 | tf_op jit(solution)/shard_map/all_gather | solution.py:47
  180.4 5.9 %fusion.18 = bf16[8,256,512]{2,1,0:T(8,128)(2,1)} fusion(bf16[1024,512,1]{0,1,2:T(8,128)(2,1)S(1)} %bitcast.67, bf16[16,1024,256]{2,1,0:T(8,128)(2,1)} %bitcast.75, s32[]{:T(128)S(6)} %select_n.19), kind=kOutput, calls=%fused_computation.21 | convolution fusion | flops 2148532224 | bytes 7340036 | tf_op jit(solution)/shard_map/htf,tc->hfc/dot_general | solution.py:55
  186.3 1.5 collective-permute-start
  187.8 1.1 dynamic-slice_bitcast_fusion
  188.9 1.1 dynamic-slice_bitcast_fusion.1
  190.0 0.1 maximum_bitcast_fusion
  190.1 0.0 slice-start
  190.1 1.1 copy.61
  191.2 0.0 slice-start.1
  191.2 0.0 collective-permute-done.1
  191.2 5.2 %add_multiply_fusion = f32[8,256,512]{2,1,0:T(8,128)S(1)} fusion(bf16[8,256,512]{2,1,0:T(8,128)(2,1)S(1)} %collective-permute-done.1, bf16[1024,512,1]{0,1,2:T(8,128)(2,1)S(1)} %bitcast.68, bf16[16,1024,256]{2,1,0:T(8,128)(2,1)} %bitcast.74, s32[]{:T(128)S(6)} %select_n.18), kind=kOutput, calls=%fused_computation.10 | convolution fusion | flops 2150629376 | bytes 11534340 | tf_op jit(solution)/shard_map/htf,tc->hfc/dot_general | solution.py:55
  196.3 38.1 %collective-permute-done = bf16[8,256,512]{2,1,0:T(8,128)(2,1)} collective-permute-done((bf16[8,256,512]{2,1,0:T(8,128)(2,1)}, bf16[8,256,512]{2,1,0:T(8,128)(2,1)}, u32[]{:S(2)}, u32[]{:S(2)}) %collective-permute-start) | collective-permute-done | bytes 2097184 | tf_op jit(solution)/shard_map/ppermute | solution.py:61
  234.4 0.0 slice-done
  234.4 0.0 slice-done.1
  234.4 4.0 %add_multiply_fusion.1 = f32[8,256,512]{2,1,0:T(8,128)S(1)} fusion(bf16[8,256,512]{2,1,0:T(8,128)(2,1)} %collective-permute-done, bf16[1024,512,1]{0,1,2:T(8,128)(2,1)S(1)} %bitcast.69, bf16[16,1024,256]{2,1,0:T(8,128)(2,1)S(1)} %bitcast.79, s32[]{:T(128)S(6)} %select_n.18), kind=kOutput, calls=%fused_computation.15 | convolution fusion | flops 2150629376 | bytes 11534340 | tf_op jit(solution)/shard_map/htf,tc->hfc/dot_general | solution.py:55
  238.4 0.0 copy-start.1
  238.5 5.1 %pad_maximum_fusion = f32[8,512,512]{2,1,0:T(8,128)} fusion(f32[8,256,512]{2,1,0:T(8,128)S(1)} %add_multiply_fusion, f32[8,256,512]{2,1,0:T(8,128)S(1)} %add_multiply_fusion.1), kind=kLoop, calls=%fused_computation.5 | loop fusion | flops 2097152 | bytes 16777216 | tf_op jit(solution)/shard_map/concatenate | solution.py:67
  243.6 0.0 copy-done.1
  (1 shorter events, 0.0 us)
Async XLA Ops:
  7.2 1.9 copy-start
  7.2 98.2 %all-gather.7.cloned.1.call-start = ((), (), s32[]{:S(2)}) async-start(), calls=%async_computation.1 | async-start | bytes 8912896 | tf_op jit(solution)/shard_map/all_gather | solution.py:47
  28.2 152.3 %all-gather.5.cloned.1.call-start = ((), (), s32[]{:S(2)}) async-start(), calls=%async_computation | async-start | bytes 8912896 | tf_op jit(solution)/shard_map/all_gather | solution.py:47
  111.3 79.9 %collective-permute-start.1 = (bf16[8,256,512]{2,1,0:T(8,128)(2,1)}, bf16[8,256,512]{2,1,0:T(8,128)(2,1)S(1)}, u32[]{:S(2)}, u32[]{:S(2)}) collective-permute-start(bf16[8,256,512]{2,1,0:T(8,128)(2,1)} %fusion.21), channel_id=1, source_target_pairs={{0,16},{16,0},{1,17},{17,1},{2,18},{18,2},{3,19},{19,3},{4,20},{20... | collective-permute-start | bytes 6291464 | tf_op jit(solution)/shard_map/ppermute | solution.py:61
  186.3 48.1 %collective-permute-start = (bf16[8,256,512]{2,1,0:T(8,128)(2,1)}, bf16[8,256,512]{2,1,0:T(8,128)(2,1)}, u32[]{:S(2)}, u32[]{:S(2)}) collective-permute-start(bf16[8,256,512]{2,1,0:T(8,128)(2,1)} %fusion.18), channel_id=1, source_target_pairs={{0,16},{16,0},{1,17},{17,1},{2,18},{18,2},{3,19},{19,3},{4,20},{20... | collective-permute-start | bytes 6291464 | tf_op jit(solution)/shard_map/ppermute | solution.py:61
  190.1 44.3 %slice-start = ((s8[8388608]{0:T(1024)(128)(4,1)}), s8[4194304]{0:T(1024)(128)(4,1)S(1)}, s32[]{:S(2)}) async-start(s8[8388608]{0:T(1024)(128)(4,1)} %bitcast.77), calls=%async_computation.2 | async-start | bytes 8388608
  191.2 43.3 %slice-start.1 = ((s8[8388608]{0:T(1024)(128)(4,1)}), s8[4194304]{0:T(1024)(128)(4,1)S(1)}, s32[]{:S(2)}) async-start(s8[8388608]{0:T(1024)(128)(4,1)} %bitcast.77), calls=%async_computation.3 | async-start | bytes 8388608
  238.4 5.1 %copy-start.1 = (bf16[1024,512]{1,0:T(8,128)(2,1)S(1)}, bf16[1024,512]{1,0:T(8,128)(2,1)}, u32[]{:S(2)}) copy-start(bf16[1024,512]{1,0:T(8,128)(2,1)} %param.4) | copy-start | bytes 3145732
Sparse Core Ops, SparseCore 0:
  28.3 77.0 all-gather.6
  107.5 72.8 all-gather.4

commit v2 on v0

--- a/solution.py
+++ b/solution.py
@@ -1,11 +1,15 @@
+import functools
 import math
 
 import jax
 import jax.numpy as jnp
 from jax import lax
+from jax.experimental import pallas as pl
+from jax.experimental.pallas import tpu as pltpu
 from jax.sharding import PartitionSpec as P
 
 HEAD_SIZE = 128
+MESH = pl.DeviceIdType.MESH
 
 
 def attend(queries, keys, values):
@@ -30,21 +34,290 @@
     return attended_values.astype(jnp.bfloat16).reshape(rows_local, heads_local * HEAD_SIZE)
 
 
-def gram_block(left_part, right_part):
-    return lax.dot_general(
-        left_part, right_part, (((0,), (0,)), ((), ())), preferred_element_type=jnp.float32
-    )
+def exchange_kernel(
+    groups, heads, scale,
+    own_ref, regrouped_ref, hessian_ref,
+    gathered, total, leaving, arrived,
+    ring_send, ring_recv, pair_send, pair_recv, sum_send, sum_recv,
+    load_sem, rows_sem, out_sem,
+):
+    rows, cols = own_ref.shape
+    half = rows // 2
+    chips = heads // 2
+    depth = chips // 2
+    per_group = heads // groups
+    rows_out = rows // heads
+    tile = min(cols, 256)
+    me = lax.axis_index("dp")
+    here = lax.axis_index("head")
+    core = lax.rem(here, 2)
+    chip = lax.div(here, 2)
+    layers = chips // 2
+    side = lax.rem(chip, 2)
+    level = lax.div(chip, 2)
+    place = level + side * (2 * layers - 1 - 2 * level)
+
+    def head_at(position, which):
+        spot = lax.rem(position + 2 * chips, chips)
+        far = lax.div(spot, layers)
+        height = spot + far * (2 * layers - 1 - 2 * spot)
+        return (height * 2 + far) * 2 + which
+
+    right = head_at(place + 1, core)
+    left = head_at(place - 1, core)
+    partner = here + 1 - 2 * core
+
+    load = pltpu.make_async_copy(own_ref, gathered.at[here], load_sem)
+    load.start()
+    barrier = pltpu.get_barrier_semaphore()
+    for other in (right, left, partner):
+        pl.semaphore_signal(barrier, inc=1, device_id=(me, other), device_id_type=MESH)
+    for shift in range(1, groups):
+        pl.semaphore_signal(
+            barrier, inc=1, device_id=(lax.rem(me + shift, groups), here), device_id_type=MESH
+        )
+    pl.semaphore_wait(barrier, 3 + groups - 1)
+    load.wait()
+
+    def block(head, part):
+        return gathered.at[head, pl.ds(part * half, half)]
+
+    def ring(direction, part, step):
+        source = head_at(place + step * (2 * direction - 1), core)
+        ref = block(source, part)
+        return pltpu.make_async_remote_copy(
+            src_ref=ref, dst_ref=ref,
+            send_sem=ring_send.at[direction, part, step],
+            recv_sem=ring_recv.at[direction, part, step],
+            device_id=(me, right if direction == 0 else left), device_id_type=MESH,
+        )
+
+    def ring_arrival(direction, part, step):
+        source = head_at(place + step * (2 * direction - 1), core)
+        ref = block(source, part)
+        return pltpu.make_async_remote_copy(
+            src_ref=ref, dst_ref=ref,
+            send_sem=ring_send.at[direction, part, step - 1],
+            recv_sem=ring_recv.at[direction, part, step - 1],
+            device_id=(me, right if direction == 0 else left), device_id_type=MESH,
+        )
+
+    def pair(direction, part, step, which):
+        ref = block(head_at(place + step * (2 * direction - 1), which), part)
+        return pltpu.make_async_remote_copy(
+            src_ref=ref, dst_ref=ref,
+            send_sem=pair_send.at[direction, part, step],
+            recv_sem=pair_recv.at[direction, part, step],
+            device_id=(me, partner), device_id_type=MESH,
+        )
+
+    def sum_copy(shift, local):
+        return pltpu.make_async_remote_copy(
+            src_ref=leaving.at[shift - 1, local], dst_ref=arrived.at[shift - 1, local],
+            send_sem=sum_send.at[shift - 1, local], recv_sem=sum_recv.at[shift - 1, local],
+            device_id=(lax.rem(me + shift, groups), here), device_id_type=MESH,
+        )
+
+    def rows_copy(head):
+        return pltpu.make_async_copy(
+            gathered.at[head, pl.ds(pl.multiple_of(here * rows_out, rows_out), rows_out)],
+            regrouped_ref.at[:, pl.ds(pl.multiple_of(head * cols, cols), cols)],
+            rows_sem.at[head],
+        )
+
+    def out_copy(local):
+        return pltpu.make_async_copy(
+            total.at[local],
+            hessian_ref.at[pl.ds(pl.multiple_of(local * cols, cols), cols)],
+            out_sem.at[local],
+        )
+
+    def gram(head):
+        rows_copy(head).start()
+        owner = lax.div(head, per_group)
+        local = lax.rem(head, per_group)
+        shift = lax.rem(owner - me + groups, groups)
+
+        def one(t, carry):
+            where = pl.ds(pl.multiple_of(t * tile, tile), tile)
+            term = lax.dot_general(
+                gathered[head, :, where], gathered[here],
+                (((0,), (0,)), ((), ())), preferred_element_type=jnp.float32,
+            )
+
+            @pl.when(shift == 0)
+            def _():
+                total[local, where] = term
+
+            @pl.when(shift != 0)
+            def _():
+                leaving[shift - 1, local, where] = term.astype(jnp.bfloat16)
+
+            return carry
+
+        lax.fori_loop(0, cols // tile, one, 0)
+
+        @pl.when(shift != 0)
+        def _():
+            sum_copy(shift, local).start()
+
+    reach = {(0, 0): depth, (1, 0): depth - 1, (0, 1): depth - 1, (1, 1): depth}
+    for part in range(2):
+        for direction in range(2):
+            ring(direction, part, 0).start()
+    for part in range(2):
+        pair(0, part, 0, core).start()
+    gram(here)
+
+    def receive(part, step):
+        for direction in range(2):
+            ring_arrival(direction, part, step).wait_recv()
+            if reach[direction, part] == depth:
+                ring(direction, part, step).start()
+            else:
+                @pl.when(step < depth - 1)
+                def _():
+                    ring(direction, part, step).start()
+            pair(direction, part, step, core).start()
+
+    def pair_arrivals(step):
+        for part in range(2):
+            for direction in range(2):
+                pair(direction, part, step, 1 - core).wait_recv()
+
+    def advance(step, carry):
+        receive(0, step)
+
+        @pl.when(step == 1)
+        def _():
+            for part in range(2):
+                pair(0, part, 0, 1 - core).wait_recv()
+            gram(partner)
+
+        @pl.when(step > 1)
+        def _():
+            pair_arrivals(step - 1)
+            gram(head_at(place - step + 1, 1 - core))
+            gram(head_at(place + step - 1, 1 - core))
+
+        receive(1, step)
+        gram(head_at(place - step, core))
+        gram(head_at(place + step, core))
+        return carry
+
+    lax.fori_loop(1, depth, advance, 0)
+    for direction, part in ((0, 0), (1, 1)):
+        ring_arrival(direction, part, depth).wait_recv()
+        pair(direction, part, depth, core).start()
+    if depth > 1:
+        pair_arrivals(depth - 1)
+        gram(head_at(place - depth + 1, 1 - core))
+        gram(head_at(place + depth - 1, 1 - core))
+    gram(head_at(place - depth, core))
+    for direction, part in ((0, 0), (1, 1)):
+        pair(direction, part, depth, 1 - core).wait_recv()
+    gram(head_at(place - depth, 1 - core))
+
+    def finish(order, carry):
+        away = lax.div(order, 4)
+        kind = lax.rem(order, 4)
+        head = head_at(
+            place + (away + 1) * (2 * lax.rem(kind, 2) - 1), lax.rem(core + lax.div(kind, 2), 2)
+        )
+        collect(head)
+        return carry
+
+    def collect(head):
+        owner = lax.div(head, per_group)
+        local = lax.rem(head, per_group)
+
+        @pl.when(owner == me)
+        def _():
+            for shift in range(1, groups):
+                sum_copy(shift, local).wait_recv()
+            value = total[local]
+            for shift in range(1, groups):
+                value = value + arrived[shift - 1, local].astype(jnp.float32)
+            total[local] = value * scale
+            out_copy(local).start()
+
+    collect(here)
+    collect(partner)
+    lax.fori_loop(0, 4 * (depth - 1), finish, 0)
+    collect(head_at(place - depth, core))
+    collect(head_at(place - depth, 1 - core))
+
+    def drain(head, carry):
+        rows_copy(head).wait()
+        owner = lax.div(head, per_group)
+        local = lax.rem(head, per_group)
+        shift = lax.rem(owner - me + groups, groups)
+
+        @pl.when(shift != 0)
+        def _():
+            sum_copy(shift, local).wait_send()
+
+        @pl.when(shift == 0)
+        def _():
+            out_copy(local).wait()
+
+        return carry
+
+    lax.fori_loop(0, heads, drain, 0)
+
+    def drain_sends(step, carry):
+        for (direction, part), distance in reach.items():
+            @pl.when(step < distance)
+            def _():
+                ring(direction, part, step).wait_send()
+
+            @pl.when((step > 0) & (step <= distance))
+            def _():
+                pair(direction, part, step, core).wait_send()
+        return carry
+
+    lax.fori_loop(0, depth + 1, drain_sends, 0)
+    for part in range(2):
+        pair(0, part, 0, core).wait_send()
+
+
+def exchange(outputs, groups, heads):
+    rows, cols = outputs.shape
+    per_group = heads // groups
+    depth = heads // 4
+    dma = pltpu.SemaphoreType.DMA
+    return pl.pallas_call(
+        functools.partial(exchange_kernel, groups, heads, 2.0 / (rows * groups)),
+        out_shape=(
+            jax.ShapeDtypeStruct((rows // heads, heads * cols), jnp.bfloat16),
+            jax.ShapeDtypeStruct((per_group * cols, cols), jnp.float32),
+        ),
+        in_specs=[pl.BlockSpec(memory_space=pl.ANY)],
+        out_specs=(pl.BlockSpec(memory_space=pl.ANY), pl.BlockSpec(memory_space=pl.ANY)),
+        scratch_shapes=[
+            pltpu.VMEM((heads, rows, cols), jnp.bfloat16),
+            pltpu.VMEM((per_group, cols, cols), jnp.float32),
+            pltpu.VMEM((groups - 1, per_group, cols, cols), jnp.bfloat16),
+            pltpu.VMEM((groups - 1, per_group, cols, cols), jnp.bfloat16),
+            dma((2, 2, depth)),
+            dma((2, 2, depth)),
+            dma((2, 2, depth + 1)),
+            dma((2, 2, depth + 1)),
+            dma((groups - 1, per_group)),
+            dma((groups - 1, per_group)),
+            dma,
+            dma((heads,)),
+            dma((per_group,)),
+        ],
+        compiler_params=pltpu.CompilerParams(
+            collective_id=0, has_side_effects=True, vmem_limit_bytes=56 * 1024 * 1024
+        ),
+    )(outputs)
 
 
 def body(queries, keys, values):
     outputs = attend(queries, keys, values)
-    rows_local = outputs.shape[0]
-    regrouped = lax.all_to_all(outputs, "head", split_axis=0, concat_axis=1, tiled=True)
-    term = gram_block(lax.all_gather(outputs, "head", axis=1, tiled=True), outputs)
-    summed = lax.psum_scatter(term, "dp", scatter_dimension=0, tiled=True)
-    tokens_all = rows_local * lax.axis_size("dp")
-    hessian = summed * (2.0 / tokens_all)
-    return (regrouped, hessian)
+    return exchange(outputs, lax.axis_size("dp"), lax.axis_size("head"))
 
 
 def solution(mesh):

time: 376 us -> 175 us (0.47)
  waiting for transfers between devices: 286 us -> 0 us
  Pallas kernels: 0 us -> 142 us
  blocking collectives: 27.4 us -> 0 us
  matrix products: 34.9 us -> 18 us
  between operations: 14.1 us -> 0.68 us
  local copies, waits for them, and re-layouts: 4.95 us -> 12.8 us
  other arithmetic: 8.13 us -> 0.31 us
    reduce_scatter x1 -> x0, waiting for transfers between devices: 157 us -> none  [body(): summed = lax.psum_scatter(term, 'dp', scatter_dimension=0, tiled=True)]
    pallas_call x0 -> x1, Pallas kernels: none -> 142 us  [exchange(): pl.pallas_call(functools.partial(exchange_kernel, groups, heads, 2.0 / (r...]
    all_gather x1 -> x0, waiting for transfers between devices: 129 us -> none  [body(): lax.all_gather(outputs, 'head', axis=1, tiled=True)]
    all_to_all x1 -> x0, blocking collectives: 27.4 us -> none  [body(): lax.all_to_all(outputs, 'head', split_axis=0, concat_axis=1, tiled=True)]
    dot_general x1 -> x0, matrix products: 16 us -> none  [gram_block(): lax.dot_general(left_part, right_part, (((0,), (0,)), ((), ())), preferre...]
    unnamed x6, local copies, waits for them, and re-layouts: 1.21 us -> 10.9 us
    mul x1 -> x0, other arithmetic: 7.82 us -> none  [body(): hessian = summed * (2.0 / tokens_all)]
  transfers between devices with their start and end apart: 2 -> 0, of which waited for: 2 -> 0; matrix products, arithmetic and copies ran while one was open for 0% -> 0% of each run, Pallas kernels for 0% -> 0%
where the time goes in v2:
time: 175 us; the launch traced here: 174 us
  Pallas kernels  142 us (81%)
  matrix products  18 us (10%)
  local copies, waits for them, and re-layouts  12.8 us (7%)
    pallas_call x1, Pallas kernels, exchange(): pl.pallas_call(functools.partial(exchange_kernel, groups, heads, 2.0 / (r...  142 us
    unnamed x6, local copies, waits for them, and re-layouts  10.9 us
    sub x1, matrix products, attend(): raised = jnp.exp(logit_matrix - peak)  10.9 us
    dot_general x1, matrix products, attend(): jnp.einsum('hqk,khd->qhd', attention_weight, value_heads, preferred_eleme...  7.06 us

profile of v2, /device:TPU:0, one launch (start us, length us, event | category | flops | bytes accessed | tf_op | source)
XLA Modules:
  0.0 174.1 jit_solution(4068652536805485752)
XLA Ops:
  0.6 0.0 copy-start
  0.6 0.0 copy-start.1
  0.7 0.3 iota_compare_fusion
  1.0 0.9 copy-done
  1.9 10.9 %fusion.30 = (f32[4,1024]{1,0:T(4,128)S(1)}, f32[4,1024,1024]{1,2,0:T(8,128)}) fusion(pred[1024,1024]{0,1:T(8,128)(4,1)S(1)} %iota_compare_fusion, bf16[1024,512]{1,0:T(8,128)(2,1)S(1)} %copy-done, bf16[1024,512]{1,0:T(8,128)(2,1)} %param.3), kind=kOutput, calls=%fused_computation.23 | convolution fusion | flops 1090520064 | bytes 19939328 | tf_op jit(solution)/shard_map/sub | solution.py:29
  12.8 0.0 copy-done.1
  12.8 0.5 copy.11
  13.3 7.1 %fusion.8 = bf16[4,1024,128]{1,2,0:T(8,128)(2,1)S(1)} fusion(bf16[1024,4,128]{0,2,1:T(8,128)(2,1)S(1)} %bitcast.46, f32[4,1024,1024]{1,2,0:T(8,128)} %get-tuple-element.3, f32[4,1024]{1,0:T(4,128)S(1)} %get-tuple-element.2), kind=kOutput, calls=%fused_computation.11 | convolution fusion | flops 1082654720 | bytes 18890752 | tf_op jit(solution)/shard_map/hqk,khd->qhd/dot_general | solution.py:31
  20.4 1.3 copy.12.own_ref
  21.7 142.3 %shard_map.50 = (bf16[64,8192]{1,0:T(8,128)(2,1)}, f32[4096,512]{1,0:T(8,128)}) custom-call(bf16[1024,512]{1,0:T(8,128)(2,1)} %copy.12.own_ref), custom_call_target="tpu_custom_call" | custom-call | tf_op jit(solution)/shard_map/pallas_call | solution.py:289
  164.0 2.3 %copy.49 = bf16[64,8192]{1,0:T(8,128)(2,1)} copy(bf16[64,8192]{1,0:T(8,128)(2,1)} %get-tuple-element.6) | data formatting | bytes 2097152
  166.3 7.8 %copy.50 = f32[4096,512]{1,0:T(8,128)} copy(f32[4096,512]{1,0:T(8,128)} %get-tuple-element.7) | data formatting | bytes 16777216
Async XLA Ops:
  0.6 1.2 copy-start
  0.6 12.1 %copy-start.1 = (bf16[1024,512]{1,0:T(8,128)(2,1)S(1)}, bf16[1024,512]{1,0:T(8,128)(2,1)}, u32[]{:S(2)}) copy-start(bf16[1024,512]{1,0:T(8,128)(2,1)} %param.5) | copy-start | bytes 3145732

commit v3 on v2

--- a/solution.py
+++ b/solution.py
@@ -12,37 +12,16 @@
 MESH = pl.DeviceIdType.MESH
 
 
-def attend(queries, keys, values):
-    rows_local = queries.shape[0]
-    heads_local = queries.shape[1] // HEAD_SIZE
-    query_heads = queries.reshape(rows_local, heads_local, HEAD_SIZE)
-    key_heads = keys.reshape(rows_local, heads_local, HEAD_SIZE)
-    value_heads = values.reshape(rows_local, heads_local, HEAD_SIZE)
-    logit_matrix = jnp.einsum(
-        "qhd,khd->hqk", query_heads, key_heads, preferred_element_type=jnp.float32
-    ) * (1.0 / math.sqrt(HEAD_SIZE))
-    causal = lax.broadcasted_iota(jnp.int32, (rows_local, rows_local), 0) >= lax.broadcasted_iota(
-        jnp.int32, (rows_local, rows_local), 1
-    )
-    logit_matrix = jnp.where(causal[None], logit_matrix, -1e30)
-    peak = jnp.max(logit_matrix, axis=-1, keepdims=True)
-    raised = jnp.exp(logit_matrix - peak)
-    attention_weight = (raised / jnp.sum(raised, axis=-1, keepdims=True)).astype(jnp.bfloat16)
-    attended_values = jnp.einsum(
-        "hqk,khd->qhd", attention_weight, value_heads, preferred_element_type=jnp.float32
-    )
-    return attended_values.astype(jnp.bfloat16).reshape(rows_local, heads_local * HEAD_SIZE)
-
-
 def exchange_kernel(
     groups, heads, scale,
-    own_ref, regrouped_ref, hessian_ref,
-    gathered, total, leaving, arrived,
+    query_ref, key_ref, value_ref, regrouped_ref, total,
+    gathered, leaving, arrived,
     ring_send, ring_recv, pair_send, pair_recv, sum_send, sum_recv,
-    load_sem, rows_sem, out_sem,
+    rows_sem,
 ):
-    rows, cols = own_ref.shape
+    rows, cols = query_ref.shape
     half = rows // 2
+    quarter = rows // 4
     chips = heads // 2
     depth = chips // 2
     per_group = heads // groups
@@ -67,8 +46,6 @@
     left = head_at(place - 1, core)
     partner = here + 1 - 2 * core
 
-    load = pltpu.make_async_copy(own_ref, gathered.at[here], load_sem)
-    load.start()
     barrier = pltpu.get_barrier_semaphore()
     for other in (right, left, partner):
         pl.semaphore_signal(barrier, inc=1, device_id=(me, other), device_id_type=MESH)
@@ -76,8 +53,29 @@
         pl.semaphore_signal(
             barrier, inc=1, device_id=(lax.rem(me + shift, groups), here), device_id_type=MESH
         )
-    pl.semaphore_wait(barrier, 3 + groups - 1)
-    load.wait()
+
+    def attend(part):
+        def head_of(index, carry):
+            lanes = pl.ds(pl.multiple_of(index * HEAD_SIZE, HEAD_SIZE), HEAD_SIZE)
+            for strip in range(2 * part, 2 * part + 2):
+                seen = (strip + 1) * quarter
+                here_rows = pl.ds(strip * quarter, quarter)
+                logits = lax.dot_general(
+                    query_ref[here_rows, lanes], key_ref[pl.ds(0, seen), lanes],
+                    (((1,), (1,)), ((), ())), preferred_element_type=jnp.float32,
+                ) * (1.0 / math.sqrt(HEAD_SIZE))
+                row = lax.broadcasted_iota(jnp.int32, logits.shape, 0) + strip * quarter
+                column = lax.broadcasted_iota(jnp.int32, logits.shape, 1)
+                logits = jnp.where(row >= column, logits, -1e30)
+                raised = jnp.exp(logits - jnp.max(logits, axis=-1, keepdims=True))
+                weight = raised * (1.0 / jnp.sum(raised, axis=-1, keepdims=True))
+                gathered[here, here_rows, lanes] = jnp.dot(
+                    weight.astype(jnp.bfloat16), value_ref[pl.ds(0, seen), lanes],
+                    preferred_element_type=jnp.float32,
+                ).astype(jnp.bfloat16)
+            return carry
+
+        lax.fori_loop(0, cols // HEAD_SIZE, head_of, 0)
 
     def block(head, part):
         return gathered.at[head, pl.ds(part * half, half)]
@@ -125,13 +123,6 @@
             rows_sem.at[head],
         )
 
-    def out_copy(local):
-        return pltpu.make_async_copy(
-            total.at[local],
-            hessian_ref.at[pl.ds(pl.multiple_of(local * cols, cols), cols)],
-            out_sem.at[local],
-        )
-
     def gram(head):
         rows_copy(head).start()
         owner = lax.div(head, per_group)
@@ -163,9 +154,11 @@
 
     reach = {(0, 0): depth, (1, 0): depth - 1, (0, 1): depth - 1, (1, 1): depth}
     for part in range(2):
+        attend(part)
+        if part == 0:
+            pl.semaphore_wait(barrier, 3 + groups - 1)
         for direction in range(2):
             ring(direction, part, 0).start()
-    for part in range(2):
         pair(0, part, 0, core).start()
     gram(here)
 
@@ -239,7 +232,6 @@
             for shift in range(1, groups):
                 value = value + arrived[shift - 1, local].astype(jnp.float32)
             total[local] = value * scale
-            out_copy(local).start()
 
     collect(here)
     collect(partner)
@@ -257,10 +249,6 @@
         def _():
             sum_copy(shift, local).wait_send()
 
-        @pl.when(shift == 0)
-        def _():
-            out_copy(local).wait()
-
         return carry
 
     lax.fori_loop(0, heads, drain, 0)
@@ -281,22 +269,22 @@
         pair(0, part, 0, core).wait_send()
 
 
-def exchange(outputs, groups, heads):
-    rows, cols = outputs.shape
+def exchange(queries, keys, values, groups, heads):
+    rows, cols = queries.shape
     per_group = heads // groups
     depth = heads // 4
     dma = pltpu.SemaphoreType.DMA
+    vmem = pl.BlockSpec(memory_space=pltpu.VMEM)
     return pl.pallas_call(
         functools.partial(exchange_kernel, groups, heads, 2.0 / (rows * groups)),
         out_shape=(
-            jax.ShapeDtypeStruct((rows // heads, heads * cols), jnp.bfloat16),
-            jax.ShapeDtypeStruct((per_group * cols, cols), jnp.float32),
+            pltpu.VMEM((rows // heads, heads * cols), jnp.bfloat16),
+            pltpu.VMEM((per_group, cols, cols), jnp.float32),
         ),
-        in_specs=[pl.BlockSpec(memory_space=pl.ANY)],
-        out_specs=(pl.BlockSpec(memory_space=pl.ANY), pl.BlockSpec(memory_space=pl.ANY)),
+        in_specs=[vmem, vmem, vmem],
+        out_specs=(vmem, vmem),
         scratch_shapes=[
             pltpu.VMEM((heads, rows, cols), jnp.bfloat16),
-            pltpu.VMEM((per_group, cols, cols), jnp.float32),
             pltpu.VMEM((groups - 1, per_group, cols, cols), jnp.bfloat16),
             pltpu.VMEM((groups - 1, per_group, cols, cols), jnp.bfloat16),
             dma((2, 2, depth)),
@@ -305,19 +293,20 @@
             dma((2, 2, depth + 1)),
             dma((groups - 1, per_group)),
             dma((groups - 1, per_group)),
-            dma,
             dma((heads,)),
-            dma((per_group,)),
         ],
         compiler_params=pltpu.CompilerParams(
-            collective_id=0, has_side_effects=True, vmem_limit_bytes=56 * 1024 * 1024
+            collective_id=0, has_side_effects=True, vmem_limit_bytes=40 * 1024 * 1024
         ),
-    )(outputs)
+    )(queries, keys, values)
 
 
 def body(queries, keys, values):
-    outputs = attend(queries, keys, values)
-    return exchange(outputs, lax.axis_size("dp"), lax.axis_size("head"))
+    cols = queries.shape[1]
+    regrouped, total = exchange(
+        queries, keys, values, lax.axis_size("dp"), lax.axis_size("head")
+    )
+    return (regrouped, total.reshape(-1, cols))
 
 
 def solution(mesh):

time: 175 us -> 154 us (0.88)
  matrix products: 18 us -> 0 us
  local copies, waits for them, and re-layouts: 12.8 us -> 8.04 us
  Pallas kernels: 142 us -> 145 us
    sub x1 -> x0, matrix products: 10.9 us -> none  [attend(): raised = jnp.exp(logit_matrix - peak)]
    dot_general x1 -> x0, matrix products: 7.06 us -> none  [attend(): jnp.einsum('hqk,khd->qhd', attention_weight, value_heads, preferred_eleme...]
    unnamed x6 -> x8, local copies, waits for them, and re-layouts: 10.9 us -> 8.04 us
    pallas_call x1, Pallas kernels: 142 us -> 145 us  [exchange(): pl.pallas_call(functools.partial(exchange_kernel, groups, heads, 2.0 / (r...]
    reshape x2 -> x0, local copies, waits for them, and re-layouts: 1.85 us -> none  [the longest x1 1.32 us: attend(): attended_values.astype(jnp.bfloat16)]
where the time goes in v3:
time: 154 us
  Pallas kernels  145 us (94%)
  local copies, waits for them, and re-layouts  8.04 us (5%)
    pallas_call x1, Pallas kernels, exchange(): pl.pallas_call(functools.partial(exchange_kernel, groups, heads, 2.0 / (r...  145 us
    unnamed x8, local copies, waits for them, and re-layouts  8.04 us

profile of v3, /device:TPU:0, one launch (start us, length us, event | category | flops | bytes accessed | tf_op | source)
XLA Modules:
  0.0 153.9 jit_solution(7941835271732326090)
XLA Ops:
  0.6 0.0 copy-start
  0.6 1.2 copy-done
  1.9 0.0 copy-start.1
  1.9 1.2 copy-done.1
  3.1 0.0 copy-start.2
  3.1 1.2 copy-done.2
  4.3 145.2 %shard_map.50 = (bf16[64,8192]{1,0:T(8,128)(2,1)S(1)}, f32[8,512,512]{2,1,0:T(8,128)S(1)}) custom-call(bf16[1024,512]{1,0:T(8,128)(2,1)S(1)} %copy-done, bf16[1024,512]{1,0:T(8,128)(2,1)S(1)} %copy-done.1, bf16[1024,512]{1,0:T(8,128)(2,1)S(1)} %copy-done.2), custom_call_target="tpu_custom_call" | custom-call | tf_op jit(solution)/shard_map/pallas_call | solution.py:278
  149.5 1.0 copy.7
  150.5 3.4 %copy.8 = f32[4096,512]{1,0:T(8,128)} copy(f32[4096,512]{1,0:T(8,128)S(1)} %bitcast.1) | data formatting | bytes 16777216
Async XLA Ops:
  0.6 1.2 copy-start
  1.9 1.2 copy-start.1
  3.1 1.2 copy-start.2

commit v4 on v3

--- a/solution.py
+++ b/solution.py
@@ -14,10 +14,10 @@
 
 def exchange_kernel(
     groups, heads, scale,
-    query_ref, key_ref, value_ref, regrouped_ref, total,
-    gathered, leaving, arrived,
+    query_hbm, key_hbm, value_hbm, regrouped_ref, total,
+    query_ref, key_ref, value_ref, gathered, leaving, arrived, lent,
     ring_send, ring_recv, pair_send, pair_recv, sum_send, sum_recv,
-    rows_sem,
+    rows_sem, load_sem, lent_send,
 ):
     rows, cols = query_ref.shape
     half = rows // 2
@@ -46,7 +46,22 @@
     left = head_at(place - 1, core)
     partner = here + 1 - 2 * core
 
+    loads = [
+        pltpu.make_async_copy(source, target, load_sem.at[n])
+        for n, (source, target) in enumerate(
+            ((query_hbm, query_ref), (key_hbm, key_ref), (value_hbm, value_ref))
+        )
+    ]
+    for load in loads:
+        load.start()
+    lending = groups == 2
+    lends = level == (layers - 1) * me
+    borrows = level == (layers - 1) * (1 - me)
+    mirror = ((layers - 1 - level) * 2 + side) * 2 + core
+
     barrier = pltpu.get_barrier_semaphore()
+    if lending:
+        pl.semaphore_signal(barrier, inc=1, device_id=(1 - me, mirror), device_id_type=MESH)
     for other in (right, left, partner):
         pl.semaphore_signal(barrier, inc=1, device_id=(me, other), device_id_type=MESH)
     for shift in range(1, groups):
@@ -152,11 +167,48 @@
         def _():
             sum_copy(shift, local).start()
 
+    def lent_copy(which):
+        local = lax.rem((level * 2 + 1 - side) * 2 + which, per_group)
+        return pltpu.make_async_remote_copy(
+            src_ref=lent.at[which], dst_ref=arrived.at[0, local],
+            send_sem=lent_send.at[which], recv_sem=sum_recv.at[0, local],
+            device_id=(1 - me, mirror), device_id_type=MESH,
+        )
+
+    def gram_for_mirror(which):
+        head = (level * 2 + 1 - side) * 2 + which
+
+        def one(t, carry):
+            where = pl.ds(pl.multiple_of(t * tile, tile), tile)
+            lent[which, where] = lax.dot_general(
+                gathered[head, :, where], gathered[mirror],
+                (((0,), (0,)), ((), ())), preferred_element_type=jnp.float32,
+            ).astype(jnp.bfloat16)
+            return carry
+
+        lax.fori_loop(0, cols // tile, one, 0)
+        lent_copy(which).start()
+
+    def gram_far(head):
+        if not lending:
+            gram(head)
+            return
+
+        @pl.when(lends)
+        def _():
+            rows_copy(head).start()
+
+        @pl.when(jnp.logical_not(lends))
+        def _():
+            gram(head)
+
     reach = {(0, 0): depth, (1, 0): depth - 1, (0, 1): depth - 1, (1, 1): depth}
+    for load in loads:
+        load.wait()
     for part in range(2):
         attend(part)
         if part == 0:
-            pl.semaphore_wait(barrier, 3 + groups - 1)
+            pl.semaphore_wait(barrier, 3 + groups - 1 + int(lending))
         for direction in range(2):
             ring(direction, part, 0).start()
         pair(0, part, 0, core).start()
@@ -206,10 +258,15 @@
         pair_arrivals(depth - 1)
         gram(head_at(place - depth + 1, 1 - core))
         gram(head_at(place + depth - 1, 1 - core))
-    gram(head_at(place - depth, core))
+    gram_far(head_at(place - depth, core))
     for direction, part in ((0, 0), (1, 1)):
         pair(direction, part, depth, 1 - core).wait_recv()
-    gram(head_at(place - depth, 1 - core))
+    gram_far(head_at(place - depth, 1 - core))
+    if lending:
+        @pl.when(borrows)
+        def _():
+            for which in range(2):
+                gram_for_mirror(which)
 
     def finish(order, carry):
         away = lax.div(order, 4)
@@ -245,7 +302,12 @@
         local = lax.rem(head, per_group)
         shift = lax.rem(owner - me + groups, groups)
 
-        @pl.when(shift != 0)
+        sends = shift != 0
+        if lending:
+            lent_out = lends & (lax.div(head, 2) == (layers - 1 - level) * 2 + 1 - side)
+            sends = sends & jnp.logical_not(lent_out)
+
+        @pl.when(sends)
         def _():
             sum_copy(shift, local).wait_send()
 
@@ -267,6 +329,11 @@
     lax.fori_loop(0, depth + 1, drain_sends, 0)
     for part in range(2):
         pair(0, part, 0, core).wait_send()
+    if lending:
+        @pl.when(borrows)
+        def _():
+            for which in range(2):
+                lent_copy(which).wait_send()
 
 
 def exchange(queries, keys, values, groups, heads):
@@ -281,12 +348,16 @@
             pltpu.VMEM((rows // heads, heads * cols), jnp.bfloat16),
             pltpu.VMEM((per_group, cols, cols), jnp.float32),
         ),
-        in_specs=[vmem, vmem, vmem],
+        in_specs=[pl.BlockSpec(memory_space=pltpu.HBM)] * 3,
         out_specs=(vmem, vmem),
         scratch_shapes=[
+            pltpu.VMEM((rows, cols), jnp.bfloat16),
+            pltpu.VMEM((rows, cols), jnp.bfloat16),
+            pltpu.VMEM((rows, cols), jnp.bfloat16),
             pltpu.VMEM((heads, rows, cols), jnp.bfloat16),
             pltpu.VMEM((groups - 1, per_group, cols, cols), jnp.bfloat16),
             pltpu.VMEM((groups - 1, per_group, cols, cols), jnp.bfloat16),
+            pltpu.VMEM((2, cols, cols), jnp.bfloat16),
             dma((2, 2, depth)),
             dma((2, 2, depth)),
             dma((2, 2, depth + 1)),
@@ -294,9 +365,11 @@
             dma((groups - 1, per_group)),
             dma((groups - 1, per_group)),
             dma((heads,)),
+            dma((3,)),
+            dma((2,)),
         ],
         compiler_params=pltpu.CompilerParams(
-            collective_id=0, has_side_effects=True, vmem_limit_bytes=40 * 1024 * 1024
+            collective_id=0, has_side_effects=True, vmem_limit_bytes=109 * 512 * 1024
         ),
     )(queries, keys, values)
 

time: 154 us -> 152 us (0.987)
  local copies, waits for them, and re-layouts: 8.04 us -> 4.37 us
  Pallas kernels: 145 us -> 147 us
    unnamed x8 -> x2, local copies, waits for them, and re-layouts: 8.04 us -> 4.37 us
    pallas_call x1, Pallas kernels: 145 us -> 147 us  [exchange(): pl.pallas_call(functools.partial(exchange_kernel, groups, heads, 2.0 / (r...]
where the time goes in v4:
time: 152 us
  Pallas kernels  147 us (97%)
  local copies, waits for them, and re-layouts  4.37 us (3%)
    pallas_call x1, Pallas kernels, exchange(): pl.pallas_call(functools.partial(exchange_kernel, groups, heads, 2.0 / (r...  147 us
    unnamed x2, local copies, waits for them, and re-layouts  4.37 us

profile of v4, /device:TPU:0, one launch (start us, length us, event | category | flops | bytes accessed | tf_op | source)
XLA Modules:
  0.0 152.1 jit_solution(15450172964971514857)
XLA Ops:
  0.6 147.1 %shard_map.50 = (bf16[64,8192]{1,0:T(8,128)(2,1)S(1)}, f32[8,512,512]{2,1,0:T(8,128)S(1)}) custom-call(bf16[1024,512]{1,0:T(8,128)(2,1)} %query_hbm.1, bf16[1024,512]{1,0:T(8,128)(2,1)} %key_hbm.1, bf16[1024,512]{1,0:T(8,128)(2,1)} %value_hbm.1), custom_call_target="tpu_custom_call" | custom-call | tf_op jit(solution)/shard_map/pallas_call | solution.py:345
  147.7 1.0 copy.7
  148.7 3.4 %copy.8 = f32[4096,512]{1,0:T(8,128)} copy(f32[4096,512]{1,0:T(8,128)S(1)} %bitcast.1) | data formatting | bytes 16777216

commit v5 on v4

--- a/solution.py
+++ b/solution.py
@@ -15,9 +15,9 @@
 def exchange_kernel(
     groups, heads, scale,
     query_hbm, key_hbm, value_hbm, regrouped_ref, total,
-    query_ref, key_ref, value_ref, gathered, leaving, arrived, lent,
+    query_ref, key_ref, value_ref, gathered, leaving, arrived, lent, relayed,
     ring_send, ring_recv, pair_send, pair_recv, sum_send, sum_recv,
-    rows_sem, load_sem, lent_send,
+    rows_sem, load_sem, lent_send, lent_recv, relay_send,
 ):
     rows, cols = query_ref.shape
     half = rows // 2
@@ -61,7 +61,7 @@
 
     barrier = pltpu.get_barrier_semaphore()
     if lending:
-        pl.semaphore_signal(barrier, inc=1, device_id=(1 - me, mirror), device_id_type=MESH)
+        pl.semaphore_signal(barrier, inc=1, device_id=(me, mirror), device_id_type=MESH)
     for other in (right, left, partner):
         pl.semaphore_signal(barrier, inc=1, device_id=(me, other), device_id_type=MESH)
     for shift in range(1, groups):
@@ -168,11 +168,18 @@
             sum_copy(shift, local).start()
 
     def lent_copy(which):
+        return pltpu.make_async_remote_copy(
+            src_ref=lent.at[which], dst_ref=relayed.at[which],
+            send_sem=lent_send.at[which], recv_sem=lent_recv.at[which],
+            device_id=(1 - me, here), device_id_type=MESH,
+        )
+
+    def relay_copy(which):
         local = lax.rem((level * 2 + 1 - side) * 2 + which, per_group)
         return pltpu.make_async_remote_copy(
-            src_ref=lent.at[which], dst_ref=arrived.at[0, local],
-            send_sem=lent_send.at[which], recv_sem=sum_recv.at[0, local],
-            device_id=(1 - me, mirror), device_id_type=MESH,
+            src_ref=relayed.at[which], dst_ref=arrived.at[0, local],
+            send_sem=relay_send.at[which], recv_sem=sum_recv.at[0, local],
+            device_id=(me, mirror), device_id_type=MESH,
         )
 
     def gram_for_mirror(which):
@@ -295,6 +302,15 @@
     lax.fori_loop(0, 4 * (depth - 1), finish, 0)
     collect(head_at(place - depth, core))
     collect(head_at(place - depth, 1 - core))
+
+    if lending:
+        @pl.when(lends)
+        def _():
+            for which in range(2):
+                lent_copy(which).wait_recv()
+                relay_copy(which).start()
+            for which in range(2):
+                relay_copy(which).wait_send()
 
     def drain(head, carry):
         rows_copy(head).wait()
@@ -358,6 +374,7 @@
             pltpu.VMEM((groups - 1, per_group, cols, cols), jnp.bfloat16),
             pltpu.VMEM((groups - 1, per_group, cols, cols), jnp.bfloat16),
             pltpu.VMEM((2, cols, cols), jnp.bfloat16),
+            pltpu.VMEM((2, cols, cols), jnp.bfloat16),
             dma((2, 2, depth)),
             dma((2, 2, depth)),
             dma((2, 2, depth + 1)),
@@ -367,6 +384,8 @@
             dma((heads,)),
             dma((3,)),
             dma((2,)),
+            dma((2,)),
+            dma((2,)),
         ],
         compiler_params=pltpu.CompilerParams(
             collective_id=0, has_side_effects=True, vmem_limit_bytes=109 * 512 * 1024

time: 152 us -> 148 us (0.974); the launches traced: 152 us -> 146 us
  Pallas kernels: 147 us -> 141 us
    pallas_call x1, Pallas kernels: 147 us -> 141 us  [exchange(): pl.pallas_call(functools.partial(exchange_kernel, groups, heads, 2.0 / (r...]
where the time goes in v5:
time: 148 us; the launch traced here: 146 us
  Pallas kernels  141 us (95%)
  local copies, waits for them, and re-layouts  4.37 us (3%)
    pallas_call x1, Pallas kernels, exchange(): pl.pallas_call(functools.partial(exchange_kernel, groups, heads, 2.0 / (r...  141 us
    unnamed x2, local copies, waits for them, and re-layouts  4.37 us

profile of v5, /device:TPU:0, one launch (start us, length us, event | category | flops | bytes accessed | tf_op | source)
XLA Modules:
  0.0 145.6 jit_solution(9995379913386886282)
XLA Ops:
  0.6 140.6 %shard_map.50 = (bf16[64,8192]{1,0:T(8,128)(2,1)S(1)}, f32[8,512,512]{2,1,0:T(8,128)S(1)}) custom-call(bf16[1024,512]{1,0:T(8,128)(2,1)} %query_hbm.1, bf16[1024,512]{1,0:T(8,128)(2,1)} %key_hbm.1, bf16[1024,512]{1,0:T(8,128)(2,1)} %value_hbm.1), custom_call_target="tpu_custom_call" | custom-call | tf_op jit(solution)/shard_map/pallas_call | solution.py:361
  141.2 1.0 copy.7
  142.2 3.4 %copy.8 = f32[4096,512]{1,0:T(8,128)} copy(f32[4096,512]{1,0:T(8,128)S(1)} %bitcast.1) | data formatting | bytes 16777216

commit v6 on v5

--- a/solution.py
+++ b/solution.py
@@ -54,9 +54,10 @@
     ]
     for load in loads:
         load.start()
-    lending = groups == 2
+    lending = groups == 2 and layers >= 4
     lends = level == (layers - 1) * me
     borrows = level == (layers - 1) * (1 - me)
+    held = (level + 2 * me - 1) * 2 + 1 - side
     mirror = ((layers - 1 - level) * 2 + side) * 2 + core
 
     barrier = pltpu.get_barrier_semaphore()
@@ -163,7 +164,11 @@
 
         lax.fori_loop(0, cols // tile, one, 0)
 
-        @pl.when(shift != 0)
+        sends = shift != 0
+        if lending:
+            sends = sends & jnp.logical_not(borrows & (lax.div(head, 2) == held))
+
+        @pl.when(sends)
         def _():
             sum_copy(shift, local).start()
 
@@ -253,6 +258,14 @@
             gram(head_at(place + step - 1, 1 - core))
 
         receive(1, step)
+        if lending:
+            @pl.when(borrows & (step == depth - 1))
+            def _():
+                for which in range(2):
+                    gram_for_mirror(which)
+                for which in range(2):
+                    sum_copy(1, lax.rem(held * 2 + which, per_group)).start()
+
         gram(head_at(place - step, core))
         gram(head_at(place + step, core))
         return carry
@@ -269,13 +282,15 @@
     for direction, part in ((0, 0), (1, 1)):
         pair(direction, part, depth, 1 - core).wait_recv()
     gram_far(head_at(place - depth, 1 - core))
-    if lending:
-        @pl.when(borrows)
-        def _():
-            for which in range(2):
-                gram_for_mirror(which)
 
     def finish(order, carry):
+        if lending:
+            @pl.when(lends & (order == 4))
+            def _():
+                for which in range(2):
+                    lent_copy(which).wait_recv()
+                    relay_copy(which).start()
+
         away = lax.div(order, 4)
         kind = lax.rem(order, 4)
         head = head_at(
@@ -306,9 +321,6 @@
     if lending:
         @pl.when(lends)
         def _():
-            for which in range(2):
-                lent_copy(which).wait_recv()
-                relay_copy(which).start()
             for which in range(2):
                 relay_copy(which).wait_send()
 

time: 148 us -> 135 us (0.912); the launches traced: 146 us -> 135 us
  Pallas kernels: 141 us -> 130 us
    pallas_call x1, Pallas kernels: 141 us -> 130 us  [exchange(): pl.pallas_call(functools.partial(exchange_kernel, groups, heads, 2.0 / (r...]
where the time goes in v6:
time: 135 us
  Pallas kernels  130 us (96%)
  local copies, waits for them, and re-layouts  4.37 us (3%)
    pallas_call x1, Pallas kernels, exchange(): pl.pallas_call(functools.partial(exchange_kernel, groups, heads, 2.0 / (r...  130 us
    unnamed x2, local copies, waits for them, and re-layouts  4.37 us

profile of v6, /device:TPU:0, one launch (start us, length us, event | category | flops | bytes accessed | tf_op | source)
XLA Modules:
  0.0 135.2 jit_solution(9293053478221877746)
XLA Ops:
  0.6 130.2 %shard_map.50 = (bf16[64,8192]{1,0:T(8,128)(2,1)S(1)}, f32[8,512,512]{2,1,0:T(8,128)S(1)}) custom-call(bf16[1024,512]{1,0:T(8,128)(2,1)} %query_hbm.1, bf16[1024,512]{1,0:T(8,128)(2,1)} %key_hbm.1, bf16[1024,512]{1,0:T(8,128)(2,1)} %value_hbm.1), custom_call_target="tpu_custom_call" | custom-call | tf_op jit(solution)/shard_map/pallas_call | solution.py:373
  130.9 1.0 copy.7
  131.8 3.4 %copy.8 = f32[4096,512]{1,0:T(8,128)} copy(f32[4096,512]{1,0:T(8,128)S(1)} %bitcast.1) | data formatting | bytes 16777216
